TPU v7x, 32 devices: a whole 2x2x4 slice. The times are simulated.
32 devices in a mesh: dp: 4 (over y, x), ctx: 8 (over z, core).
Axes of the slice: x: 2, y: 2, z: 4, core: 2. Of those that a mesh axis runs over, the one named last changes fastest.
Arguments:
- tokens: bfloat16 [4, 1024, 2048], P('dp', 'ctx'), may hold values from -6 to 6
- positions: int32 [4, 1024], P('dp', 'ctx'), may hold values from 0 to 1023, as said below
- norm_gain: float32 [2048], replicated, may hold values from 0.5 to 1.5
- norm_bias: float32 [2048], replicated, may hold values from -1.8 to 1.8
- qkv_weight: bfloat16 [2048, 6144], P('ctx'), may hold values from -0.125 to 0.125
- qkv_bias: float32 [6144], replicated, may hold values from -1.8 to 1.8
- dense_weight: bfloat16 [2048, 2048], P('ctx'), may hold values from -2 to 2
- dense_bias: float32 [2048], replicated, may hold values from -1.8 to 1.8
- up_weight: bfloat16 [2048, 8192], P('ctx'), may hold values from -0.125 to 0.125
- up_bias: float32 [8192], replicated, may hold values from -1.8 to 1.8
- down_weight: bfloat16 [8192, 2048], P('ctx'), may hold values from -0.0625 to 0.0625
- down_bias: float32 [2048], replicated, may hold values from -1.8 to 1.8
- clip_limit: int32 [32], replicated, may hold values from 3 to 11
- cotangent: bfloat16 [4, 1024, 2048], P('dp', 'ctx'), may hold values from -6 to 6
Outputs:
- layer_out: bfloat16 [4, 1024, 2048], P('dp', 'ctx')
- tokens_grad: float32 [4, 1024, 2048], P('dp', 'ctx')
- norm_gain_grad: float32 [2048], replicated
- norm_bias_grad: float32 [2048], replicated
- qkv_weight_grad: float32 [2048, 6144], P('ctx')
- qkv_bias_grad: float32 [6144], replicated
- dense_weight_grad: float32 [2048, 2048], P('ctx')
- dense_bias_grad: float32 [2048], replicated
- up_weight_grad: float32 [2048, 8192], P('ctx')
- up_bias_grad: float32 [8192], replicated
- down_weight_grad: float32 [8192, 2048], P('ctx')
- down_bias_grad: float32 [2048], replicated
- head_maxima: float32 [32], replicated
- clipped_weight: float32 [2048, 4096], P('ctx')
- clipped_bias: float32 [4096], replicated
Inputs may be any that keep to these rules, and one draw needn't show every extreme that they name: `positions`: within each sequence the ids rise by one from 0 at its first token and return to 0 at the first token of each packed document; the first sequence holds a single document.
All inputs are finite; a program needn't handle non-finite values.
Results may differ from a plain program's by a relative error of at most 0.017.
Values may be sent and summed in bfloat16 or wider, within the bound.
No kernel may reach another device: no remote copies, remote signals or barrier semaphores. Data moves between devices by JAX's collectives and lax.ppermute only.
A program may use at most 512 MiB of HBM per device.

v0:
```python
from functools import partial
import jax
import jax.numpy as jnp
from jax import lax
from jax.sharding import PartitionSpec as P

ROT = 32
EPSILON = 1e-05
MASKED = -1e30
ROPE_BASE = 10000.0
BF16 = jnp.bfloat16
F32 = jnp.float32


def rotary_tables(positions):
    half_rot = ROT // 2
    frequency = ROPE_BASE ** (-(jnp.arange(half_rot, dtype=F32) * 2.0 / ROT))
    angles = positions.astype(F32)[..., None] * frequency
    cosine = jnp.cos(angles)
    sine = jnp.sin(angles)
    return (
        jnp.concatenate([cosine, cosine], -1)[..., None, :],
        jnp.concatenate([sine, sine], -1)[..., None, :],
    )


def rotate(values, cosine, sine):
    half_rot = ROT // 2
    turned = values[..., :ROT]
    swapped = jnp.concatenate([-turned[..., half_rot:], turned[..., :half_rot]], -1)
    return jnp.concatenate([turned * cosine + swapped * sine, values[..., ROT:]], -1)


def rotate_back(gradient, cosine, sine):
    half_rot = ROT // 2
    turned = gradient[..., :ROT]
    scaled = turned * sine
    swapped = jnp.concatenate([scaled[..., half_rot:], -scaled[..., :half_rot]], -1)
    return jnp.concatenate([turned * cosine + swapped, gradient[..., ROT:]], -1)


def dot(left, right, contract):
    return lax.dot_general(
        left, right, ((contract[:1], contract[1:]), ((), ())), preferred_element_type=F32
    )


def per_device(
    tokens,
    positions,
    norm_gain,
    norm_bias,
    qkv_weight,
    qkv_bias,
    dense_weight,
    dense_bias,
    up_weight,
    up_bias,
    down_weight,
    down_bias,
    clip_limit,
    cotangent,
):
    seqs, stretch, width = tokens.shape
    heads = clip_limit.shape[0]
    head_dim = width // heads
    rows = seqs * stretch
    parts = lax.axis_size("ctx")
    part = lax.axis_index("ctx")
    own_heads = heads // parts
    own = own_heads * head_dim
    own_rows = qkv_weight.shape[0]
    own_ff = down_weight.shape[0]
    length = stretch * parts
    all_rows = seqs * length
    scale = head_dim ** (-0.5)
    pieces = jnp.concatenate(
        [
            qkv_weight.reshape(own_rows, 3, parts, own)
            .transpose(2, 0, 1, 3)
            .reshape(parts, own_rows, 3 * own),
            up_weight.reshape(own_rows, parts, own_ff).transpose(1, 0, 2),
        ],
        axis=2,
    )
    in_weight = lax.all_to_all(pieces, "ctx", split_axis=0, concat_axis=0, tiled=True).reshape(
        width, 3 * own + own_ff
    )
    grad_rows = lax.all_gather(cotangent, "ctx", axis=1, tiled=True).reshape(all_rows, width)
    inputs = tokens.reshape(rows, width).astype(F32)
    centre = inputs - jnp.mean(inputs, axis=-1, keepdims=True)
    inv_std = lax.rsqrt(jnp.mean(centre * centre, axis=-1, keepdims=True) + EPSILON)
    normed = centre * inv_std
    hidden_local = (normed * norm_gain + norm_bias).astype(BF16)
    hidden = lax.all_gather(
        hidden_local.reshape(seqs, stretch, width), "ctx", axis=1, tiled=True
    ).reshape(all_rows, width)
    all_positions = lax.all_gather(positions, "ctx", axis=1, tiled=True)
    qkv_own_bias = lax.dynamic_slice_in_dim(
        qkv_bias.reshape(3, parts, own), part, 1, axis=1
    ).reshape(3 * own)
    up_own_bias = lax.dynamic_slice_in_dim(up_bias, part * own_ff, own_ff)
    projected = dot(hidden, in_weight, (1, 0))
    joined = projected[:, : 3 * own] + qkv_own_bias
    upward = projected[:, 3 * own :] + up_own_bias
    cosine, sine = rotary_tables(all_positions)
    shaped = joined.reshape(seqs, length, 3, own_heads, head_dim)
    queries = rotate(shaped[:, :, 0], cosine, sine).astype(BF16)
    keys = rotate(shaped[:, :, 1], cosine, sine).astype(BF16)
    values = shaped[:, :, 2].astype(BF16)
    place = jnp.arange(length, dtype=jnp.int32)
    allowed = place[:, None] >= place[None, :]
    scores = jnp.einsum("sqhd,skhd->shqk", queries, keys, preferred_element_type=F32) * scale
    scores = jnp.where(allowed, scores, MASKED)
    row_max = jnp.max(scores, axis=-1, keepdims=True)
    expo = jnp.exp(scores - row_max)
    row_sum = jnp.sum(expo, axis=-1, keepdims=True)
    probs = expo / row_sum
    probs_low = probs.astype(BF16)
    mixed = jnp.einsum("shqk,skhd->sqhd", probs_low, values, preferred_element_type=F32)
    attended = mixed.reshape(all_rows, own).astype(BF16)
    own_maxima = jnp.max(row_max, axis=(0, 2, 3))
    slots = lax.dynamic_update_slice_in_dim(
        jnp.full((heads,), MASKED, F32), own_maxima, part * own_heads, axis=0
    )
    head_maxima = lax.pmax(slots, ("dp", "ctx"))
    activated = jax.nn.gelu(upward, approximate=True).astype(BF16)
    branch = dot(attended, dense_weight, (1, 0)) + dot(activated, down_weight, (1, 0))
    branch_sum = lax.psum_scatter(
        branch.astype(BF16).reshape(seqs, length, width), "ctx", scatter_dimension=1, tiled=True
    ).reshape(rows, width)
    layer_out = (inputs + branch_sum.astype(F32) + dense_bias + down_bias).astype(BF16)
    mixed_grad = dot(grad_rows, dense_weight, (1, 1)).astype(BF16)
    act_grad = dot(grad_rows, down_weight, (1, 1))
    dense_grad = dot(attended, grad_rows, (0, 0))
    down_grad = dot(activated, grad_rows, (0, 0))
    out_bias_grad = jnp.sum(cotangent.reshape(rows, width).astype(F32), axis=0)
    unused_value, gelu_back = jax.vjp(partial(jax.nn.gelu, approximate=True), upward)
    up_low = gelu_back(act_grad)[0].astype(BF16)
    mixed_low = mixed_grad.reshape(seqs, length, own_heads, head_dim)
    value_grad = jnp.einsum("shqk,sqhd->skhd", probs_low, mixed_low, preferred_element_type=F32)
    prob_grad = jnp.einsum("sqhd,skhd->shqk", mixed_low, values, preferred_element_type=F32)
    delta = jnp.sum(probs * prob_grad, axis=-1, keepdims=True)
    score_grad = (probs * (prob_grad - delta)).astype(BF16)
    query_grad = jnp.einsum("shqk,skhd->sqhd", score_grad, keys, preferred_element_type=F32) * scale
    key_grad = (
        jnp.einsum("shqk,sqhd->skhd", score_grad, queries, preferred_element_type=F32) * scale
    )
    joined_low = (
        jnp.stack(
            [
                rotate_back(query_grad, cosine, sine),
                rotate_back(key_grad, cosine, sine),
                value_grad,
            ],
            axis=2,
        )
        .reshape(all_rows, 3 * own)
        .astype(BF16)
    )
    both = jnp.concatenate([joined_low, up_low], axis=1)
    hidden_part = dot(both, in_weight, (1, 1))
    hidden_grad = (
        lax.psum_scatter(
            hidden_part.astype(BF16).reshape(seqs, length, width),
            "ctx",
            scatter_dimension=1,
            tiled=True,
        )
        .reshape(rows, width)
        .astype(F32)
    )
    in_grad = dot(hidden, both, (0, 0)).astype(BF16)
    in_quarter = lax.psum_scatter(
        in_grad.reshape(parts, own_rows, 3 * own + own_ff), "dp", scatter_dimension=1, tiled=True
    )
    in_quarter = lax.all_to_all(in_quarter, "ctx", split_axis=0, concat_axis=0, tiled=True)
    in_rows = lax.all_gather(in_quarter.transpose(1, 0, 2), "dp", axis=0, tiled=True)
    qkv_grad = (
        in_rows[:, :, : 3 * own]
        .reshape(own_rows, parts, 3, own)
        .transpose(0, 2, 1, 3)
        .reshape(own_rows, 3 * width)
        .astype(F32)
    )
    up_grad = in_rows[:, :, 3 * own :].reshape(own_rows, parts * own_ff).astype(F32)
    out_grad = lax.psum(jnp.concatenate([dense_grad, down_grad], axis=0).astype(BF16), "dp")
    gain_part = jnp.sum(hidden_grad * normed, axis=0)
    shift_part = jnp.sum(hidden_grad, axis=0)
    scaled = hidden_grad * norm_gain
    tokens_grad = cotangent.reshape(rows, width).astype(F32) + inv_std * (
        scaled
        - jnp.mean(scaled, axis=-1, keepdims=True)
        - normed * jnp.mean(scaled * normed, axis=-1, keepdims=True)
    )
    qkv_bias_part = lax.dynamic_update_slice(
        jnp.zeros((3, parts, own), F32),
        jnp.sum(joined_low.astype(F32), axis=0).reshape(3, 1, own),
        (0, part, 0),
    ).reshape(3 * width)
    up_bias_part = lax.dynamic_update_slice(
        jnp.zeros((parts * own_ff,), F32), jnp.sum(up_low.astype(F32), axis=0), (part * own_ff,)
    )
    gain_grad, shift_grad, qkv_bias_grad, out_bias_grad, up_bias_grad = lax.psum(
        (gain_part, shift_part, qkv_bias_part, out_bias_grad, up_bias_part), ("dp", "ctx")
    )
    limits = clip_limit.astype(F32)
    factor = limits / jnp.maximum(head_maxima, limits)
    column_scale = jnp.tile(jnp.repeat(jnp.sqrt(factor), head_dim), 2)
    clipped_weight = qkv_weight[:, : 2 * width].astype(F32) * column_scale
    clipped_bias = qkv_bias[: 2 * width] * column_scale
    return (
        layer_out.reshape(seqs, stretch, width),
        tokens_grad.reshape(seqs, stretch, width),
        gain_grad,
        shift_grad,
        qkv_grad,
        qkv_bias_grad,
        out_grad[:own].astype(F32),
        out_bias_grad,
        up_grad,
        up_bias_grad,
        out_grad[own:].astype(F32),
        out_bias_grad,
        head_maxima,
        clipped_weight,
        clipped_bias,
    )


def solution(mesh):
    rows = P("dp", "ctx", None)
    weight = P("ctx", None)
    in_specs = (rows, P("dp", "ctx"), P(), P()) + (weight, P()) * 4 + (P(), rows)
    out_specs = (rows, rows, P(), P()) + (weight, P()) * 4 + (P(), weight, P())
    return jax.shard_map(
        per_device, mesh=mesh, in_specs=in_specs, out_specs=out_specs, check_vma=False
    )
```

profile of v0, /device:TPU:0, one launch (start us, length us, event | category | flops | bytes accessed | tf_op | source)
XLA Modules:
  0.0 971.7 jit_solution(4422547686251745322)
XLA Ops:
  7.9 4.6 copy.74
  16.4 6.4 copy.76
  22.9 6.7 pad_maximum_fusion
  29.6 6.5 all-to-all-start
  38.6 174.2 %all_gather.13 = s32[1,1024]{1,0:T(1,128)S(1)} all-gather(s32[1,128]{1,0:T(1,128)S(1)} %copy-done.37), channel_id=1, replica_groups=mesh['dp'=4,'ctx'=8] {'ctx'}, dimensions={1}, use_global_device_ids=true | all-gather | bytes 4608 | tf_op jit(solution)/shard_map/all_gather | solution.py:98
  214.9 4.6 fusion.47
  219.5 29.4 %all-to-all-done = bf16[8,256,1792]{1,2,0:T(8,128)(2,1)} async-done(((bf16[8,256,1792]{1,2,0:T(8,128)(2,1)}), bf16[8,256,1792]{1,2,0:T(8,128)(2,1)}, u32[]{:S(2)}, u32[]{:S(2)}) %all-to-all-start) | async-done | bytes 7340064 | tf_op jit(solution)/shard_map/all_to_all | solution.py:86
  248.9 9.9 %copy.77 = bf16[8,256,1792]{2,1,0:T(8,128)(2,1)} copy(bf16[8,256,1792]{1,2,0:T(8,128)(2,1)} %all-to-all-done) | data formatting | bytes 14680064 | tf_op jit(solution)/shard_map/all_to_all | solution.py:86
  258.9 11.6 %fusion.22 = f32[1024,1792]{1,0:T(8,128)S(1)} fusion(bf16[2048,1792]{1,0:T(8,128)(2,1)} %bitcast.151, bf16[1,1024,2048]{2,1,0:T(8,128)(2,1)} %all-gather.4.cloned.1.call-done), kind=kOutput, calls=%fused_computation.37 | convolution fusion | flops 7516192768 | bytes 18874368 | tf_op jit(solution)/shard_map/dot_general | solution.py:43
  281.1 10.4 %fusion.95 = (f32[4,1024]{1,0:T(4,128)S(1)}, f32[4,1024,1024]{1,2,0:T(8,128)}) fusion(pred[1024,1024]{0,1:T(8,128)(4,1)S(1)} %iota_compare_fusion, bf16[1024,4,32]{0,2,1:T(8,128)(2,1)S(1)} %get-tuple-element.118, bf16[1024,4,32]{0,2,1:T(8,128)(2,1)S(1)} %get-tuple-element.104, bf16[1024,4,32]{0,2,1:T(8,128)(2,1)S(1)} %get-tuple-element.117, ...), kind=kOutput, calls=%fused_computation.150 | convolution fusion | flops 555746304 | bytes 18890752 | tf_op jit(solution)/shard_map/sub | solution.py:116
  291.6 9.6 fusion.37
  301.2 15.9 %multiply_reduce_fusion = (f32[4,1024]{1,0:T(4,128)S(1)}, f32[4,1024,1024]{1,2,0:T(8,128)}) fusion(f32[4,1024,1024]{1,2,0:T(8,128)} %get-tuple-element.112, f32[4,1024]{1,0:T(4,128)S(1)} %get-tuple-element.111, bf16[1024,4,64]{0,2,1:T(8,128)(2,1)} %bitcast.164, f32[1,1024,3,4,64]{1,4,3,2,0:T(8,128)} %bitcast.148), kind=kOutput, calls=%fused_computation.2 | convolution fusion | flops 549449728 | bytes 34635776 | tf_op jit(solution)/shard_map/sqhd,skhd->shqk/dot_general | solution.py:142
  317.1 8.0 multiply_convert_fusion
  332.5 12.3 %convert_reduce_fusion = (f32[1024]{0:T(1024)}, bf16[1024,1024]{1,0:T(8,128)(2,1)S(1)}) fusion(f32[1024]{0:T(1024)S(1)} %copy-done.35, f32[1024,1792]{1,0:T(8,128)} %copy-done.5, bf16[1024,2048]{1,0:T(8,128)(2,1)} %param.24, bf16[1,1024,2048]{2,1,0:T(8,128)(2,1)} %all-gather.6.cloned.1.call-done), kind=kOutput, calls=%fused_computation.40 | convolution fusion | flops 4319083520 | bytes 14688256 | tf_op jit(solution)/shard_map/dot_general | solution.py:43
  344.8 8.5 convolution_convert_fusion
  353.3 7.0 copy.84
  360.4 12.0 %convert_bitcast_fusion.1 = bf16[1,1024,2048]{2,1,0:T(8,128)(2,1)} fusion(bf16[2048,1792]{1,0:T(8,128)(2,1)} %bitcast.152, bf16[1024,1024]{1,0:T(8,128)(2,1)} %copy-done.42, bf16[1024,768]{1,0:T(8,128)(2,1)S(1)} %copy-done.4), kind=kOutput, calls=%fused_computation.41 | convolution fusion | flops 7525629952 | bytes 15204352 | tf_op jit(solution)/shard_map/dot_general | solution.py:43
  373.4 9.1 fusion.44
  382.5 8.5 fusion.92
  398.2 8.8 fusion.28
  409.9 38.0 %reduce-scatter.8.cloned.1.call-done = bf16[8,64,1792]{2,0,1:T(8,128)(2,1)} async-done(((bf16[8,256,1792]{2,0,1:T(8,128)(2,1)}), bf16[8,64,1792]{2,0,1:T(8,128)(2,1)}) %reduce-scatter.8.cloned.1.call-update) | async-done | bytes 1835024 | tf_op jit(solution)/shard_map/reduce_scatter | solution.py:174
  456.7 78.3 %reduce-scatter.6.cloned.1.call-done = bf16[1,128,2048]{2,1,0:T(8,128)(2,1)} async-done(((bf16[1,1024,2048]{2,1,0:T(8,128)(2,1)}), bf16[1,128,2048]{2,1,0:T(8,128)(2,1)}) %reduce-scatter.6.cloned.1.call-update) | async-done | bytes 524304 | tf_op jit(solution)/shard_map/reduce_scatter | solution.py:164
  537.1 53.5 %reduce-scatter.4.cloned.1.call-done = bf16[1,128,2048]{2,1,0:T(8,128)(2,1)} async-done(((bf16[1,1024,2048]{2,1,0:T(8,128)(2,1)}), bf16[1,128,2048]{2,1,0:T(8,128)(2,1)}) %reduce-scatter.4.cloned.1.call-update) | async-done | bytes 524304 | tf_op jit(solution)/shard_map/reduce_scatter | solution.py:129
  597.0 5.4 fusion.1
  602.5 38.0 %pmax.7 = f32[32]{0:T(128)S(1)} all-reduce(f32[32]{0:T(128)S(1)} %dynamic_update_slice.11), channel_id=1, replica_groups=mesh['dp'=4,'ctx'=8] {'dp','ctx'}, use_global_device_ids=true, to_apply=%region_22.23 | all-reduce | flops 32 | bytes 256 | tf_op jit(solution)/shard_map/pmax | solution.py:126
  645.5 69.2 %all-reduce.4.cloned.1.call-done = bf16[1280,2048]{1,0:T(8,128)(2,1)} async-done(((bf16[1280,2048]{1,0:T(8,128)(2,1)}), bf16[1280,2048]{1,0:T(8,128)(2,1)}) %all-reduce.4.cloned.1.call-update) | async-done | bytes 5242896 | tf_op jit(solution)/shard_map/psum | solution.py:187
  717.5 6.7 slice_convert_fusion
  724.1 120.5 %all-reduce.6.cloned.1.call-done = (f32[2048]{0:T(1024)}, f32[2048]{0:T(1024)}, f32[6144]{0:T(1024)}, f32[2048]{0:T(1024)}, f32[8192]{0:T(1024)}) async-done(((f32[2048]{0:T(1024)}, f32[2048]{0:T(1024)}, f32[6144]{0:T(1024)}, f32[2048]{0:T(1024)}, f32[8192]{0:T(1024)}), (f32[2048]{0:T(1024)}, f32[2048]{0:T(1024)}, f32[6144]{0:T(1024)}, f32[2048]{0:T(1024)}, f32[8192]{0:T(1024)})) %all-reduce.6.cloned.1.call-update) | async-done | bytes 81936 | tf_op jit(solution)/shard_map/psum | solution.py:204
  844.6 82.7 %all-gather.8.cloned.1.call-done = bf16[256,8,1792]{2,1,0:T(8,128)(2,1)} async-done(((bf16[64,8,1792]{2,1,0:T(8,128)(2,1)}), bf16[256,8,1792]{2,1,0:T(8,128)(2,1)}) %all-gather.8.cloned.1.call-update) | async-done | bytes 7340048 | tf_op jit(solution)/shard_map/all_gather | solution.py:178
  931.1 5.0 copy.94
  939.3 11.0 %copy.96 = f32[32,8,8,1024]{3,1,2,0:T(8,128)} copy(f32[32,8,8,1024]{3,2,1,0:T(8,128)S(1)} %bitcast.139) | data formatting | bytes 16777216
  954.4 6.6 copy.89
  (181 shorter events, 77.4 us)
Async XLA Ops:
  7.2 207.7 %copy-start = (bf16[256,2048]{1,0:T(8,128)(2,1)S(1)}, bf16[256,2048]{1,0:T(8,128)(2,1)}, u32[]{:S(2)}) copy-start(bf16[256,2048]{1,0:T(8,128)(2,1)} %param.20) | copy-start | bytes 3145732
  7.2 207.7 %all-gather.6.cloned.1.call-start = ((), (), s32[]{:S(2)}) async-start(), calls=%async_computation.7 | async-start | bytes 4718592 | tf_op jit(solution)/shard_map/all_gather | solution.py:89
  29.6 183.3 %copy-start.21 = (f32[6144]{0:T(1024)S(1)}, f32[6144]{0:T(1024)}, u32[]{:S(2)}) copy-start(f32[6144]{0:T(1024)} %param.19) | copy-start | bytes 73732
  29.6 219.4 %all-to-all-start = ((bf16[8,256,1792]{1,2,0:T(8,128)(2,1)}), bf16[8,256,1792]{1,2,0:T(8,128)(2,1)}, u32[]{:S(2)}, u32[]{:S(2)}) async-start(bf16[8,256,1792]{1,2,0:T(8,128)(2,1)} %pad_maximum_fusion), calls=%async_computation | async-start | bytes 14680064 | tf_op jit(solution)/shard_map/all_to_all | solution.py:86
  36.1 222.8 %all-gather.4.cloned.1.call-start = ((), (), s32[]{:S(2)}) async-start(), calls=%async_computation.5 | async-start | bytes 4718592 | tf_op jit(solution)/shard_map/all_gather | solution.py:95
  38.6 409.4 %reduce-scatter.8.cloned.1.call-start = ((), (), s32[]{:S(2)}) async-start(), calls=%async_computation.9 | async-start | bytes 9175040 | tf_op jit(solution)/shard_map/reduce_scatter | solution.py:174
  214.9 76.7 %copy-start.6 = (pred[1024,1024]{0,1:T(8,128)(4,1)}, pred[1024,1024]{0,1:T(8,128)(4,1)S(1)}, u32[]{:S(2)}) copy-start(pred[1024,1024]{0,1:T(8,128)(4,1)S(1)} %iota_compare_fusion) | copy-start | bytes 3145732
  280.8 92.2 %copy-start.7 = (bf16[1024,4,32]{0,2,1:T(8,128)(2,1)}, bf16[1024,4,32]{0,2,1:T(8,128)(2,1)S(1)}, u32[]{:S(2)}) copy-start(bf16[1024,4,32]{0,2,1:T(8,128)(2,1)S(1)} %get-tuple-element.117) | copy-start | bytes 786436
  301.2 15.9 %slice-start = ((s8[16777216]{0:T(1024)(128)(4,1)}), s8[4194304]{0:T(1024)(128)(4,1)S(1)}, s32[]{:S(2)}) async-start(s8[16777216]{0:T(1024)(128)(4,1)} %bitcast.142), calls=%async_computation.13 | async-start | bytes 8388608
  301.2 15.9 %slice-start.1 = ((s8[16777216]{0:T(1024)(128)(4,1)}), s8[4194304]{0:T(1024)(128)(4,1)S(1)}, s32[]{:S(2)}) async-start(s8[16777216]{0:T(1024)(128)(4,1)} %bitcast.142), calls=%async_computation.14 | async-start | bytes 8388608
  301.2 15.9 %slice-start.2 = ((s8[16777216]{0:T(1024)(128)(4,1)}), s8[4194304]{0:T(1024)(128)(4,1)S(1)}, s32[]{:S(2)}) async-start(s8[16777216]{0:T(1024)(128)(4,1)} %bitcast.142), calls=%async_computation.15 | async-start | bytes 8388608
  301.2 15.9 %slice-start.3 = ((s8[16777216]{0:T(1024)(128)(4,1)}), s8[4194304]{0:T(1024)(128)(4,1)S(1)}, s32[]{:S(2)}) async-start(s8[16777216]{0:T(1024)(128)(4,1)} %bitcast.142), calls=%async_computation.16 | async-start | bytes 8388608
  332.5 12.3 %copy-start.4 = (bf16[1024,768]{1,0:T(8,128)(2,1)S(1)}, bf16[1024,768]{1,0:T(8,128)(2,1)}, u32[]{:S(2)}) copy-start(bf16[1024,768]{1,0:T(8,128)(2,1)} %copy.83) | copy-start | bytes 4718596
  332.5 12.3 %copy-start.39 = (bf16[1,1024,2048]{2,1,0:T(8,128)(2,1)S(1)}, bf16[1,1024,2048]{2,1,0:T(8,128)(2,1)}, u32[]{:S(2)}) copy-start(bf16[1,1024,2048]{2,1,0:T(8,128)(2,1)} %all-gather.4.cloned.1.call-done) | copy-start | bytes 12582916
  360.3 174.7 %reduce-scatter.6.cloned.1.call-start = ((), (), s32[]{:S(2)}) async-start(), calls=%async_computation.8 | async-start | bytes 4718592 | tf_op jit(solution)/shard_map/reduce_scatter | solution.py:164
  372.4 218.2 %reduce-scatter.4.cloned.1.call-start = ((), (), s32[]{:S(2)}) async-start(), calls=%async_computation.6 | async-start | bytes 4718592 | tf_op jit(solution)/shard_map/reduce_scatter | solution.py:129
  394.4 320.3 %all-reduce.4.cloned.1.call-start = ((), (), s32[]{:S(2)}) async-start(), calls=%async_computation.11 | async-start | bytes 10485760 | tf_op jit(solution)/shard_map/psum | solution.py:187
  409.9 46.6 %copy-start.36 = (f32[1024]{0:T(1024)S(1)}, f32[1024]{0:T(1024)}, u32[]{:S(2)}) copy-start(f32[1024]{0:T(1024)} %get-tuple-element.115) | copy-start | bytes 12292
  409.9 125.1 %copy-start.2 = (bf16[1,128,2048]{2,1,0:T(8,128)(2,1)S(1)}, bf16[1,128,2048]{2,1,0:T(8,128)(2,1)}, u32[]{:S(2)}) copy-start(bf16[1,128,2048]{2,1,0:T(8,128)(2,1)} %param.14) | copy-start | bytes 1572868
  409.9 125.1 %copy-start.20 = (f32[2048]{0:T(1024)S(1)}, f32[2048]{0:T(1024)}, u32[]{:S(2)}) copy-start(f32[2048]{0:T(1024)} %param.16) | copy-start | bytes 24580
  409.9 125.1 %copy-start.27 = (f32[128]{0:T(128)S(1)}, f32[128]{0:T(128)}, u32[]{:S(2)}) copy-start(f32[128]{0:T(128)} %copy-done.26) | copy-start | bytes 1540
  409.9 125.1 %copy-start.34 = (f32[128]{0:T(128)S(1)}, f32[128]{0:T(128)}, u32[]{:S(2)}) copy-start(f32[128]{0:T(128)} %copy-done.33) | copy-start | bytes 1540
  409.9 180.8 %copy-start.29 = (f32[2048]{0:T(1024)S(1)}, f32[2048]{0:T(1024)}, u32[]{:S(2)}) copy-start(f32[2048]{0:T(1024)} %param.25) | copy-start | bytes 24580
  409.9 180.7 %copy-start.30 = (f32[2048]{0:T(1024)S(1)}, f32[2048]{0:T(1024)}, u32[]{:S(2)}) copy-start(f32[2048]{0:T(1024)} %param.21) | copy-start | bytes 24580
  451.0 143.6 %all-to-all-start.1 = ((bf16[8,64,1792]{2,1,0:T(8,128)(2,1)}), bf16[8,64,1792]{2,1,0:T(8,128)(2,1)S(1)}, u32[]{:S(2)}, u32[]{:S(2)}) async-start(bf16[8,64,1792]{2,1,0:T(8,128)(2,1)} %copy.85), calls=%async_computation.4 | async-start | bytes 3670016 | tf_op jit(solution)/shard_map/all_to_all | solution.py:177
  455.6 389.0 %all-reduce.6.cloned.1.call-start = ((), (), s32[]{:S(2)}) async-start(), calls=%async_computation.12 | async-start | bytes 163840 | tf_op jit(solution)/shard_map/psum | solution.py:204
  456.7 137.9 %copy-start.18 = (f32[8192]{0:T(1024)}, f32[8192]{0:T(1024)S(1)}, u32[]{:S(2)}) copy-start(f32[8192]{0:T(1024)S(1)} %dynamic_update_slice.10) | copy-start | bytes 98308
  594.6 332.7 %all-gather.8.cloned.1.call-start = ((), (), s32[]{:S(2)}) async-start(), calls=%async_computation.10 | async-start | bytes 9175040 | tf_op jit(solution)/shard_map/all_gather | solution.py:178
  597.0 43.6 %copy-start.40 = (s32[32]{0:T(128)S(1)}, s32[32]{0:T(128)}, u32[]{:S(2)}) copy-start(s32[32]{0:T(128)} %param.26) | copy-start | bytes 388
  597.0 43.7 %copy-start.22 = (f32[6144]{0:T(1024)S(1)}, f32[6144]{0:T(1024)}, u32[]{:S(2)}) copy-start(f32[6144]{0:T(1024)} %param.19) | copy-start | bytes 73732
  640.5 76.9 %copy-start.41 = (f32[32]{0:T(128)}, f32[32]{0:T(128)S(1)}, u32[]{:S(2)}) copy-start(f32[32]{0:T(128)S(1)} %pmax.7) | copy-start | bytes 388
  939.3 11.0 %copy-start.3 = (bf16[256,8,768]{0,2,1:T(8,128)(2,1)S(1)}, bf16[256,8,768]{0,2,1:T(8,128)(2,1)}, u32[]{:S(2)}) copy-start(bf16[256,8,768]{0,2,1:T(8,128)(2,1)} %copy.94) | copy-start | bytes 9437188
  (25 other events, 141.7 us)
Sparse Core Ops, SparseCore 0:
  9.6 67.6 all-gather.5
  79.5 135.0 all-gather.3
  360.5 87.4 reduce-scatter.7
  450.7 84.2 reduce-scatter.5
  537.7 52.9 reduce-scatter.3
  594.4 120.2 all-reduce.3
  722.2 122.3 all-reduce.5
  847.1 80.2 all-gather.7
where the time goes:
time: 976 us; the launch traced here: 972 us
  waiting for transfers between devices  473 us (48%)
  blocking collectives  212 us (22%)
  matrix products  128 us (13%)
  local copies, waits for them, and re-layouts  84.9 us (9%)
  other arithmetic  47 us (5%)
  between operations  15 us (2%)
  starting transfers between devices  12 us (1%)
    all_gather x1, blocking collectives, per_device(): all_positions = lax.all_gather(positions, 'ctx', axis=1, tiled=True)  174 us
    psum x1, waiting for transfers between devices, per_device(): lax.psum((gain_part, shift_part, qkv_bias_part, out_bias_grad, up_bias_pa...  121 us
    all_gather x1, waiting for transfers between devices, per_device(): lax.all_gather(in_quarter.transpose(1, 0, 2), 'dp', axis=0, tiled=True)  82.7 us
    reduce_scatter x1, waiting for transfers between devices, per_device(): lax.psum_scatter(hidden_part.astype(BF16).reshape(seqs, length, width), '...  78.3 us
    dot_general x9, matrix products, dot(): lax.dot_general(left, right, ((contract[:1], contract[1:]), ((), ())), pr...  73.4 us
    psum x1, waiting for transfers between devices, per_device(): lax.psum(jnp.concatenate([dense_grad, down_grad], axis=0).astype(BF16), '...  69.2 us
    reduce_scatter x1, waiting for transfers between devices, per_device(): lax.psum_scatter(branch.astype(BF16).reshape(seqs, length, width), 'ctx',...  53.5 us
    unnamed x108, local copies, waits for them, and re-layouts  42.9 us
  transfers between devices with their start and end apart: 10, of which 7 were waited for; matrix products, arithmetic and copies ran while one was open for 12% of the time, Pallas kernels for 0%

commit v1 on v0

--- a/solution.py
+++ b/solution.py
@@ -175,7 +175,17 @@
         in_grad.reshape(parts, own_rows, 3 * own + own_ff), "dp", scatter_dimension=1, tiled=True
     )
     in_quarter = lax.all_to_all(in_quarter, "ctx", split_axis=0, concat_axis=0, tiled=True)
-    in_rows = lax.all_gather(in_quarter.transpose(1, 0, 2), "dp", axis=0, tiled=True)
+    value = in_quarter.transpose(1, 0, 2)
+    ways = lax.axis_size("dp")
+    up = [(d, (d + 1) % ways) for d in range(ways)]
+    down = [(d, (d - 1) % ways) for d in range(ways)]
+    earlier, later = ([value], [value])
+    for _ in range(ways // 2):
+        earlier.append(lax.ppermute(earlier[-1], "dp", up))
+    for _ in range((ways - 1) // 2):
+        later.append(lax.ppermute(later[-1], "dp", down))
+    line = jnp.concatenate([*earlier[::-1], *later[1:]], axis=0)
+    in_rows = jnp.roll(line, (lax.axis_index("dp") - ways // 2) * value.shape[0], axis=0)
     qkv_grad = (
         in_rows[:, :, : 3 * own]
         .reshape(own_rows, parts, 3, own)

time: 976 us -> 931 us (0.954)
  waiting for transfers between devices: 473 us -> 316 us
  blocking collectives: 212 us -> 265 us
  local copies, waits for them, and re-layouts: 84.9 us -> 136 us
    all_gather x1 -> x0, waiting for transfers between devices: 82.7 us -> none  [per_device(): lax.all_gather(in_quarter.transpose(1, 0, 2), 'dp', axis=0, tiled=True)]
    psum x1, waiting for transfers between devices: 69.2 us -> 0.01 us  [per_device(): lax.psum(jnp.concatenate([dense_grad, down_grad], axis=0).astype(BF16), '...]
    pmax x1, blocking collectives: 38 us -> 90.4 us  [per_device(): head_maxima = lax.pmax(slots, ('dp', 'ctx'))]
    reduce_scatter x1, waiting for transfers between devices: 78.3 us -> 34.9 us  [per_device(): lax.psum_scatter(hidden_part.astype(BF16).reshape(seqs, length, width), '...]
    all_to_all x1, waiting for transfers between devices: 0.01 us -> 43.4 us  [per_device(): lax.all_to_all(in_quarter, 'ctx', split_axis=0, concat_axis=0, tiled=True)]
    concatenate x0 -> x1, local copies, waits for them, and re-layouts: none -> 33.8 us  [per_device(): jnp.roll(line, (lax.axis_index('dp') - ways // 2) * value.shape[0], axis=0)]
    ppermute x0 -> x3, local copies, waits for them, and re-layouts: none -> 14.8 us  [the longest x2 9.87 us: per_device(): earlier.append(lax.ppermute(earlier[-1], 'dp', up))]
    unnamed x108 -> x101, local copies, waits for them, and re-layouts: 42.9 us -> 36 us
  transfers between devices with their start and end apart: 10 -> 12, of which waited for: 7 -> 6; matrix products, arithmetic and copies ran while one was open for 12% -> 14% of each run, Pallas kernels for 0% -> 0%
where the time goes in v1:
time: 931 us; the launch traced here: 923 us
  waiting for transfers between devices  316 us (34%)
  blocking collectives  265 us (28%)
  local copies, waits for them, and re-layouts  136 us (15%)
  matrix products  128 us (14%)
  other arithmetic  48.2 us (5%)
  starting transfers between devices  15.7 us (2%)
  between operations  15 us (2%)
    all_gather x1, blocking collectives, per_device(): all_positions = lax.all_gather(positions, 'ctx', axis=1, tiled=True)  174 us
    psum x1, waiting for transfers between devices, per_device(): lax.psum((gain_part, shift_part, qkv_bias_part, out_bias_grad, up_bias_pa...  121 us
    pmax x1, blocking collectives, per_device(): head_maxima = lax.pmax(slots, ('dp', 'ctx'))  90.4 us
    dot_general x9, matrix products, dot(): lax.dot_general(left, right, ((contract[:1], contract[1:]), ((), ())), pr...  72.5 us
    reduce_scatter x1, waiting for transfers between devices, per_device(): lax.psum_scatter(branch.astype(BF16).reshape(seqs, length, width), 'ctx',...  48.8 us
    all_to_all x1, waiting for transfers between devices, per_device(): lax.all_to_all(in_quarter, 'ctx', split_axis=0, concat_axis=0, tiled=True)  43.4 us
    reduce_scatter x1, waiting for transfers between devices, per_device(): lax.psum_scatter(in_grad.reshape(parts, own_rows, 3 * own + own_ff), 'dp'...  36.4 us
    unnamed x101, local copies, waits for them, and re-layouts  36 us
  transfers between devices with their start and end apart: 12, of which 6 were waited for; matrix products, arithmetic and copies ran while one was open for 14% of the time, Pallas kernels for 0%

profile of v1, /device:TPU:0, one launch (start us, length us, event | category | flops | bytes accessed | tf_op | source)
XLA Modules:
  0.0 923.1 jit_solution(4840171339477497677)
XLA Ops:
  16.4 6.4 copy.76
  22.9 6.7 pad_maximum_fusion
  29.6 6.5 all-to-all-start
  38.7 174.2 %all_gather.10 = s32[1,1024]{1,0:T(1,128)S(1)} all-gather(s32[1,128]{1,0:T(1,128)S(1)} %copy-done.34), channel_id=1, replica_groups=mesh['dp'=4,'ctx'=8] {'ctx'}, dimensions={1}, use_global_device_ids=true | all-gather | bytes 4608 | tf_op jit(solution)/shard_map/all_gather | solution.py:98
  218.9 30.1 %all-to-all-done = bf16[8,256,1792]{1,2,0:T(8,128)(2,1)} async-done(((bf16[8,256,1792]{1,2,0:T(8,128)(2,1)}), bf16[8,256,1792]{1,2,0:T(8,128)(2,1)}, u32[]{:S(2)}, u32[]{:S(2)}) %all-to-all-start) | async-done | bytes 7340064 | tf_op jit(solution)/shard_map/all_to_all | solution.py:86
  248.9 10.1 %copy.77 = bf16[8,256,1792]{2,1,0:T(8,128)(2,1)} copy(bf16[8,256,1792]{1,2,0:T(8,128)(2,1)} %all-to-all-done) | data formatting | bytes 14680064 | tf_op jit(solution)/shard_map/all_to_all | solution.py:86
  259.0 11.6 %fusion.22 = f32[1024,1792]{1,0:T(8,128)S(1)} fusion(bf16[2048,1792]{1,0:T(8,128)(2,1)} %bitcast.155, bf16[1,1024,2048]{2,1,0:T(8,128)(2,1)} %all-gather.3.cloned.1.call-done), kind=kOutput, calls=%fused_computation.37 | convolution fusion | flops 7516192768 | bytes 18874368 | tf_op jit(solution)/shard_map/dot_general | solution.py:43
  281.3 9.9 %fusion.95 = (f32[4,1024]{1,0:T(4,128)S(1)}, f32[4,1024,1024]{1,2,0:T(8,128)}) fusion(pred[1024,1024]{0,1:T(8,128)(4,1)S(1)} %iota_compare_fusion, bf16[1024,4,32]{0,2,1:T(8,128)(2,1)S(1)} %get-tuple-element.118, bf16[1024,4,32]{0,2,1:T(8,128)(2,1)S(1)} %get-tuple-element.104, bf16[1024,4,32]{0,2,1:T(8,128)(2,1)S(1)} %get-tuple-element.117, ...), kind=kOutput, calls=%fused_computation.152 | convolution fusion | flops 555746304 | bytes 18890752 | tf_op jit(solution)/shard_map/sub | solution.py:116
  291.3 15.8 %multiply_reduce_fusion = (f32[4,1024]{1,0:T(4,128)S(1)}, f32[4,1024,1024]{1,2,0:T(8,128)}) fusion(f32[4,1024,1024]{1,2,0:T(8,128)} %get-tuple-element.112, f32[4,1024]{1,0:T(4,128)S(1)} %get-tuple-element.111, bf16[1024,4,64]{0,2,1:T(8,128)(2,1)} %bitcast.166, f32[1,1024,3,4,64]{1,4,3,2,0:T(8,128)} %bitcast.153), kind=kOutput, calls=%fused_computation.2 | convolution fusion | flops 549449728 | bytes 34635776 | tf_op jit(solution)/shard_map/sqhd,skhd->shqk/dot_general | solution.py:142
  307.2 8.2 multiply_convert_fusion
  319.7 10.2 %fusion.37 = bf16[1,1024,1,4,64]{1,4,3,2,0:T(8,128)(2,1)} fusion(bf16[1024,4,64]{0,2,1:T(8,128)(2,1)} %bitcast.167, f32[4,1024]{1,0:T(4,128)S(1)} %get-tuple-element.111, pred[1024,1024]{0,1:T(8,128)(4,1)} %copy-done.5, bf16[1024,4,32]{0,2,1:T(8,128)(2,1)} %copy-done.8, bf16[1024,4,32]{0,2,1:T(8,128)(2,1)} %copy-done.13, ...), kind=kOutput, calls=%fused_computation.62 | convolution fusion | flops 1096815616 | bytes 3162112 | tf_op jit(solution)/shard_map/shqk,sqhd->skhd/dot_general | solution.py:141
  333.1 11.7 %convert_reduce_fusion = (f32[1024]{0:T(1024)S(1)}, bf16[1024,1024]{1,0:T(8,128)(2,1)S(1)}) fusion(f32[1024]{0:T(1024)S(1)} %dynamic_slice.11, f32[1024,1792]{1,0:T(8,128)} %copy-done.4, bf16[1024,2048]{1,0:T(8,128)(2,1)} %param.24, bf16[1,1024,2048]{2,1,0:T(8,128)(2,1)} %all-gather.5.cloned.1.call-done), kind=kOutput, calls=%fused_computation.40 | convolution fusion | flops 4319083520 | bytes 14688256 | tf_op jit(solution)/shard_map/dot_general | solution.py:43
  344.8 8.3 convolution_convert_fusion
  353.2 7.0 copy.84
  361.3 10.0 %fusion.44 = bf16[4,64,1024]{2,1,0:T(8,128)(2,1)} fusion(f32[1,1024,3,4,64]{1,4,3,2,0:T(8,128)} %bitcast.154, f32[4,1024]{1,0:T(4,128)S(1)} %get-tuple-element.111, pred[1024,1024]{0,1:T(8,128)(4,1)} %copy-done.5, bf16[1024,4,32]{0,2,1:T(8,128)(2,1)S(1)} %copy-done.10, bf16[1024,4,32]{0,2,1:T(8,128)(2,1)} %copy-done.13, ...), kind=kOutput, calls=%fused_computation.71 | convolution fusion | flops 1097077760 | bytes 3162112 | tf_op jit(solution)/shard_map/shqk,skhd->sqhd/dot_general | solution.py:120
  375.1 8.5 fusion.28
  386.7 12.5 %convert_bitcast_fusion.1 = bf16[1,1024,2048]{2,1,0:T(8,128)(2,1)} fusion(bf16[2048,1792]{1,0:T(8,128)(2,1)} %bitcast.156, bf16[1024,1024]{1,0:T(8,128)(2,1)} %copy-done.39, bf16[1024,768]{1,0:T(8,128)(2,1)S(1)} %copy-done.3), kind=kOutput, calls=%fused_computation.41 | convolution fusion | flops 7525629952 | bytes 15204352 | tf_op jit(solution)/shard_map/dot_general | solution.py:43
  399.3 8.1 fusion.92
  410.8 36.4 %reduce-scatter.8.cloned.1.call-done = bf16[8,64,1792]{2,0,1:T(8,128)(2,1)} async-done(((bf16[8,256,1792]{2,0,1:T(8,128)(2,1)}), bf16[8,64,1792]{2,0,1:T(8,128)(2,1)}) %reduce-scatter.8.cloned.1.call-update) | async-done | bytes 1835024 | tf_op jit(solution)/shard_map/reduce_scatter | solution.py:174
  454.9 43.4 %all-to-all-done.1 = bf16[8,64,1792]{2,1,0:T(8,128)(2,1)S(1)} async-done(((bf16[8,64,1792]{2,1,0:T(8,128)(2,1)}), bf16[8,64,1792]{2,1,0:T(8,128)(2,1)S(1)}, u32[]{:S(2)}, u32[]{:S(2)}) %all-to-all-start.1) | async-done | bytes 1835040 | tf_op jit(solution)/shard_map/all_to_all | solution.py:177
  506.9 90.4 %pmax.7 = f32[32]{0:T(128)S(1)} all-reduce(f32[32]{0:T(128)S(1)} %dynamic_update_slice.11), channel_id=1, replica_groups=mesh['dp'=4,'ctx'=8] {'dp','ctx'}, use_global_device_ids=true, to_apply=%region_22.23 | all-reduce | flops 32 | bytes 256 | tf_op jit(solution)/shard_map/pmax | solution.py:126
  605.8 6.7 slice_convert_fusion
  612.5 34.9 %reduce-scatter.6.cloned.1.call-done = bf16[1,128,2048]{2,1,0:T(8,128)(2,1)} async-done(((bf16[1,1024,2048]{2,1,0:T(8,128)(2,1)}), bf16[1,128,2048]{2,1,0:T(8,128)(2,1)}) %reduce-scatter.6.cloned.1.call-update) | async-done | bytes 524304 | tf_op jit(solution)/shard_map/reduce_scatter | solution.py:164
  649.5 48.8 %reduce-scatter.4.cloned.1.call-done = bf16[1,128,2048]{2,1,0:T(8,128)(2,1)} async-done(((bf16[1,1024,2048]{2,1,0:T(8,128)(2,1)}), bf16[1,128,2048]{2,1,0:T(8,128)(2,1)}) %reduce-scatter.4.cloned.1.call-update) | async-done | bytes 524304 | tf_op jit(solution)/shard_map/reduce_scatter | solution.py:129
  705.0 121.4 %all-reduce.6.cloned.1.call-done = (f32[2048]{0:T(1024)}, f32[2048]{0:T(1024)}, f32[6144]{0:T(1024)}, f32[2048]{0:T(1024)}, f32[8192]{0:T(1024)}) async-done(((f32[2048]{0:T(1024)}, f32[2048]{0:T(1024)}, f32[6144]{0:T(1024)}, f32[2048]{0:T(1024)}, f32[8192]{0:T(1024)}), (f32[2048]{0:T(1024)}, f32[2048]{0:T(1024)}, f32[6144]{0:T(1024)}, f32[2048]{0:T(1024)}, f32[8192]{0:T(1024)})) %all-reduce.6.cloned.1.call-update) | async-done | bytes 81936 | tf_op jit(solution)/shard_map/psum | solution.py:214
  829.4 4.9 copy.90
  834.3 5.0 copy.91
  839.3 4.9 copy.89
  844.2 33.8 %concatenate.102 = bf16[512,8,1792]{0,2,1:T(8,128)(2,1)} concatenate(bf16[64,8,1792]{0,2,1:T(8,128)(2,1)} %copy.89, bf16[64,8,1792]{0,2,1:T(8,128)(2,1)} %copy.90, bf16[64,8,1792]{0,2,1:T(8,128)(2,1)} %bitcast.142, bf16[64,8,1792]{0,2,1:T(8,128)(2,1)} %copy.91, bf16[64,8,1792]{0,2,1:T(8,128)(2,1)} %copy.89, bf16[64,8,1792]{0,2,1:T(8,128)(2,1)} %copy.90, ...), dimensions={0} | concatenate | bytes 29360128 | tf_op jit(solution)/shard_map/jit(_roll_dynamic)/concatenate | solution.py:188
  886.1 6.6 copy.96
  892.6 6.6 constant_dynamic-slice_fusion.1
  903.5 9.0 copy.97
  (183 shorter events, 99.5 us)
Async XLA Ops:
  7.2 207.1 %copy-start = (bf16[256,2048]{1,0:T(8,128)(2,1)S(1)}, bf16[256,2048]{1,0:T(8,128)(2,1)}, u32[]{:S(2)}) copy-start(bf16[256,2048]{1,0:T(8,128)(2,1)} %param.20) | copy-start | bytes 3145732
  7.2 207.1 %all-gather.5.cloned.1.call-start = ((), (), s32[]{:S(2)}) async-start(), calls=%async_computation.7 | async-start | bytes 4718592 | tf_op jit(solution)/shard_map/all_gather | solution.py:89
  29.6 219.4 %all-to-all-start = ((bf16[8,256,1792]{1,2,0:T(8,128)(2,1)}), bf16[8,256,1792]{1,2,0:T(8,128)(2,1)}, u32[]{:S(2)}, u32[]{:S(2)}) async-start(bf16[8,256,1792]{1,2,0:T(8,128)(2,1)} %pad_maximum_fusion), calls=%async_computation | async-start | bytes 14680064 | tf_op jit(solution)/shard_map/all_to_all | solution.py:86
  36.1 222.9 %all-gather.3.cloned.1.call-start = ((), (), s32[]{:S(2)}) async-start(), calls=%async_computation.5 | async-start | bytes 4718592 | tf_op jit(solution)/shard_map/all_gather | solution.py:95
  38.6 408.6 %reduce-scatter.8.cloned.1.call-start = ((), (), s32[]{:S(2)}) async-start(), calls=%async_computation.9 | async-start | bytes 9175040 | tf_op jit(solution)/shard_map/reduce_scatter | solution.py:174
  214.2 67.1 %copy-start.5 = (pred[1024,1024]{0,1:T(8,128)(4,1)}, pred[1024,1024]{0,1:T(8,128)(4,1)S(1)}, u32[]{:S(2)}) copy-start(pred[1024,1024]{0,1:T(8,128)(4,1)S(1)} %iota_compare_fusion) | copy-start | bytes 3145732
  281.0 34.4 %copy-start.6 = (bf16[1024,4,32]{0,2,1:T(8,128)(2,1)}, bf16[1024,4,32]{0,2,1:T(8,128)(2,1)S(1)}, u32[]{:S(2)}) copy-start(bf16[1024,4,32]{0,2,1:T(8,128)(2,1)S(1)} %get-tuple-element.117) | copy-start | bytes 786436
  281.3 34.1 %copy-start.11 = (bf16[1024,4,32]{0,2,1:T(8,128)(2,1)}, bf16[1024,4,32]{0,2,1:T(8,128)(2,1)S(1)}, u32[]{:S(2)}) copy-start(bf16[1024,4,32]{0,2,1:T(8,128)(2,1)S(1)} %get-tuple-element.103) | copy-start | bytes 786436
  291.2 15.9 %slice-start = ((s8[16777216]{0:T(1024)(128)(4,1)}), s8[4194304]{0:T(1024)(128)(4,1)S(1)}, s32[]{:S(2)}) async-start(s8[16777216]{0:T(1024)(128)(4,1)} %bitcast.146), calls=%async_computation.12 | async-start | bytes 8388608
  291.2 15.9 %slice-start.1 = ((s8[16777216]{0:T(1024)(128)(4,1)}), s8[4194304]{0:T(1024)(128)(4,1)S(1)}, s32[]{:S(2)}) async-start(s8[16777216]{0:T(1024)(128)(4,1)} %bitcast.146), calls=%async_computation.13 | async-start | bytes 8388608
  291.3 15.9 %slice-start.2 = ((s8[16777216]{0:T(1024)(128)(4,1)}), s8[4194304]{0:T(1024)(128)(4,1)S(1)}, s32[]{:S(2)}) async-start(s8[16777216]{0:T(1024)(128)(4,1)} %bitcast.146), calls=%async_computation.14 | async-start | bytes 8388608
  291.3 15.9 %slice-start.3 = ((s8[16777216]{0:T(1024)(128)(4,1)}), s8[4194304]{0:T(1024)(128)(4,1)S(1)}, s32[]{:S(2)}) async-start(s8[16777216]{0:T(1024)(128)(4,1)} %bitcast.146), calls=%async_computation.15 | async-start | bytes 8388608
  333.0 11.8 %copy-start.3 = (bf16[1024,768]{1,0:T(8,128)(2,1)S(1)}, bf16[1024,768]{1,0:T(8,128)(2,1)}, u32[]{:S(2)}) copy-start(bf16[1024,768]{1,0:T(8,128)(2,1)} %copy.83) | copy-start | bytes 4718596
  360.2 245.6 %all-reduce.4.cloned.1.call-start = ((), (), s32[]{:S(2)}) async-start(), calls=%async_computation.10 | async-start | bytes 10485760 | tf_op jit(solution)/shard_map/psum | solution.py:197
  386.5 260.9 %reduce-scatter.6.cloned.1.call-start = ((), (), s32[]{:S(2)}) async-start(), calls=%async_computation.8 | async-start | bytes 4718592 | tf_op jit(solution)/shard_map/reduce_scatter | solution.py:164
  399.3 299.0 %reduce-scatter.4.cloned.1.call-start = ((), (), s32[]{:S(2)}) async-start(), calls=%async_computation.6 | async-start | bytes 4718592 | tf_op jit(solution)/shard_map/reduce_scatter | solution.py:129
  450.2 48.1 %all-to-all-start.1 = ((bf16[8,64,1792]{2,1,0:T(8,128)(2,1)}), bf16[8,64,1792]{2,1,0:T(8,128)(2,1)S(1)}, u32[]{:S(2)}, u32[]{:S(2)}) async-start(bf16[8,64,1792]{2,1,0:T(8,128)(2,1)} %copy.85), calls=%async_computation.4 | async-start | bytes 3670016 | tf_op jit(solution)/shard_map/all_to_all | solution.py:177
  454.8 371.6 %all-reduce.6.cloned.1.call-start = ((), (), s32[]{:S(2)}) async-start(), calls=%async_computation.11 | async-start | bytes 163840 | tf_op jit(solution)/shard_map/psum | solution.py:214
  500.5 96.8 %copy-start.37 = (s32[32]{0:T(128)S(1)}, s32[32]{0:T(128)}, u32[]{:S(2)}) copy-start(s32[32]{0:T(128)} %param.26) | copy-start | bytes 388
  500.5 98.1 %copy-start.21 = (f32[6144]{0:T(1024)S(1)}, f32[6144]{0:T(1024)}, u32[]{:S(2)}) copy-start(f32[6144]{0:T(1024)} %param.19) | copy-start | bytes 73732
  500.5 105.3 %collective-permute-start = (bf16[64,8,1792]{2,1,0:T(8,128)(2,1)}, bf16[64,8,1792]{2,1,0:T(8,128)(2,1)}, u32[]{:S(2)}, u32[]{:S(2)}) collective-permute-start(bf16[64,8,1792]{2,1,0:T(8,128)(2,1)} %copy.87), channel_id=1, source_target_pairs={{0,8},{8,16},{16,24},{24,0},{1,9},{9,17},{17,25},{25,1},{2,10},{10... | collective-permute-start | bytes 5505032 | tf_op jit(solution)/shard_map/ppermute | solution.py:184
  597.3 15.2 %copy-start.38 = (f32[32]{0:T(128)}, f32[32]{0:T(128)S(1)}, u32[]{:S(2)}) copy-start(f32[32]{0:T(128)S(1)} %pmax.7) | copy-start | bytes 388
  598.6 13.8 %copy-start.17 = (f32[8192]{0:T(1024)}, f32[8192]{0:T(1024)S(1)}, u32[]{:S(2)}) copy-start(f32[8192]{0:T(1024)S(1)} %dynamic_update_slice.10) | copy-start | bytes 98308
  603.4 44.0 %copy-start.2 = (bf16[1,128,2048]{2,1,0:T(8,128)(2,1)S(1)}, bf16[1,128,2048]{2,1,0:T(8,128)(2,1)}, u32[]{:S(2)}) copy-start(bf16[1,128,2048]{2,1,0:T(8,128)(2,1)} %param.14) | copy-start | bytes 1572868
  603.4 44.0 %copy-start.19 = (f32[2048]{0:T(1024)S(1)}, f32[2048]{0:T(1024)}, u32[]{:S(2)}) copy-start(f32[2048]{0:T(1024)} %param.16) | copy-start | bytes 24580
  603.4 44.0 %copy-start.26 = (f32[128]{0:T(128)S(1)}, f32[128]{0:T(128)}, u32[]{:S(2)}) copy-start(f32[128]{0:T(128)} %copy-done.25) | copy-start | bytes 1540
  603.4 44.0 %copy-start.33 = (f32[128]{0:T(128)S(1)}, f32[128]{0:T(128)}, u32[]{:S(2)}) copy-start(f32[128]{0:T(128)} %copy-done.32) | copy-start | bytes 1540
  603.4 94.9 %copy-start.28 = (f32[2048]{0:T(1024)S(1)}, f32[2048]{0:T(1024)}, u32[]{:S(2)}) copy-start(f32[2048]{0:T(1024)} %param.25) | copy-start | bytes 24580
  603.4 94.9 %copy-start.29 = (f32[2048]{0:T(1024)S(1)}, f32[2048]{0:T(1024)}, u32[]{:S(2)}) copy-start(f32[2048]{0:T(1024)} %param.21) | copy-start | bytes 24580
  603.4 230.9 %collective-permute-start.2 = (bf16[64,8,1792]{2,1,0:T(8,128)(2,1)}, bf16[64,8,1792]{2,1,0:T(8,128)(2,1)}, u32[]{:S(2)}, u32[]{:S(2)}) collective-permute-start(bf16[64,8,1792]{2,1,0:T(8,128)(2,1)} %copy.87), channel_id=1, source_target_pairs={{0,24},{8,0},{16,8},{24,16},{1,25},{9,1},{17,9},{25,17},{2,26},{10... | collective-permute-start | bytes 5505032 | tf_op jit(solution)/shard_map/ppermute | solution.py:186
  605.8 233.5 %collective-permute-start.1 = (bf16[64,8,1792]{2,1,0:T(8,128)(2,1)}, bf16[64,8,1792]{2,1,0:T(8,128)(2,1)}, u32[]{:S(2)}, u32[]{:S(2)}) collective-permute-start(bf16[64,8,1792]{2,1,0:T(8,128)(2,1)} %collective-permute-done), channel_id=1, source_target_pairs={{0,8},{8,16},{16,24},{24,0},{1,9},{9,17},{17,25},{25,1},{2,10},{10... | collective-permute-start | bytes 5505032 | tf_op jit(solution)/shard_map/ppermute | solution.py:184
  903.4 12.0 %copy-start.22 = (f32[8192]{0:T(1024)S(1)}, f32[8192]{0:T(1024)}, u32[]{:S(2)}) copy-start(f32[8192]{0:T(1024)} %get-tuple-element.162) | copy-start | bytes 98308
  (24 other events, 145.8 us)
Sparse Core Ops, SparseCore 0:
  9.6 67.6 all-gather.4
  79.5 135.0 all-gather.2
  360.3 86.8 reduce-scatter.7
  450.9 143.8 all-reduce.3
  597.0 50.3 reduce-scatter.5
  650.1 48.1 reduce-scatter.3
  705.8 120.5 all-reduce.5
